TPU v7x, 512 devices: a whole 4x8x8 slice. The times are simulated.
512 devices in a mesh: section: 16 (over z, x_hi), expert: 32 (over x_lo, y, core).
Axes of the slice: x: 4 (x_hi: 2, x_lo: 2; x = x_hi * 2 + x_lo), y: 8, z: 8, core: 2. Of those that a mesh axis runs over, the one named last changes fastest.
Arguments:
- acts: bfloat16 [16, 4096, 3584], P('section', 'expert'), may hold values from -6 to 6
- expert_ids: int32 [16, 4096, 8], P('section', 'expert'), may hold values from 0 to 255, as said below
- gate_weights: bfloat16 [16, 4096, 8], P('section', 'expert'), may hold values from 0.049804688 to 0.34960938
- norm_gain: float32 [16, 3584], P('section'), may hold values from 0.5 to 1.5
- w_in: bfloat16 [16, 4096, 2, 3584], P('section', 'expert'), may hold values from -0.09375 to 0.09375
- w_out: bfloat16 [16, 4096, 3584], P('section', 'expert'), may hold values from -0.1875 to 0.1875
Outputs:
- advanced: bfloat16 [16, 4096, 3584], P('section', 'expert')
Inputs may be any that keep to these rules, and one draw needn't show every extreme that they name: `expert_ids`: the 8 ids of a token are distinct. Of the 128 tokens of one device, at most 24 choose any one expert below 4, and one such expert is chosen by exactly 24.
All inputs are finite; a program needn't handle non-finite values.
Results may differ from a plain program's by a relative error of at most 0.0023.
Values may be sent and summed in bfloat16 or wider, within the bound.
A program may use at most 64 MiB of HBM per device.

v0:
```python
import math

import jax
import jax.numpy as jnp
from jax import lax
from jax.sharding import PartitionSpec as P

SLICES = 8


def side_by_side(arrays, axis, split_dim, concat_dim, along):
    widths = [math.prod(a.shape[along:]) for a in arrays]
    both = jnp.concatenate(
        [a.reshape(*a.shape[:along], w) for a, w in zip(arrays, widths)], axis=along
    )
    filled = lax.all_to_all(both, axis, split_axis=split_dim, concat_axis=concat_dim, tiled=True)
    blocks = jnp.split(filled, [sum(widths[:k]) for k in range(1, len(widths))], axis=along)
    return tuple(
        (b.reshape(*filled.shape[:along], *a.shape[along:]) for a, b in zip(arrays, blocks))
    )


def from_behind(x, axis, by):
    length = lax.axis_size(axis)
    return lax.ppermute(x, axis, [(i, (i + by) % length) for i in range(length)])


def expert_work(received, w_in, w_out):
    rows, coeffs = received
    sources, items, width = rows.shape
    local_in = w_in[0]
    hid = local_in.shape[0]
    flat_rows = rows.reshape(sources * items, width)
    proj = lax.dot_general(
        flat_rows,
        local_in.reshape(hid * 2, width),
        (((1,), (1,)), ((), ())),
        preferred_element_type=jnp.float32,
    )
    proj = proj.reshape(sources * items, hid, 2)
    scale = coeffs.reshape(sources * items, 1).astype(jnp.float32)
    hidden = (scale * jax.nn.silu(proj[:, :, 0]) * proj[:, :, 1]).astype(jnp.bfloat16)
    result = jnp.dot(hidden, w_out[0], preferred_element_type=jnp.float32)
    return result.astype(jnp.bfloat16).reshape(sources, items, width)


def local(acts, expert_ids, gate_weights, norm_gain, w_in, w_out):
    tokens = acts[0]
    chosen = expert_ids[0]
    weights = gate_weights[0].astype(jnp.float32)
    tok, width = tokens.shape
    owners = lax.axis_size("expert")
    flight = owners // SLICES
    cap = 3 * tok // 16
    xf = tokens.astype(jnp.float32)
    normed = (
        xf * lax.rsqrt(jnp.mean(xf * xf, axis=-1, keepdims=True) + 1e-06) * norm_gain[0]
    ).astype(jnp.bfloat16)
    hits = chosen[:, :, None] == jnp.arange(flight, dtype=jnp.int32)[None, None, :]
    present = jnp.any(hits, axis=1).astype(jnp.int32)
    table = jnp.sum(jnp.where(hits, weights[:, :, None], jnp.float32(0.0)), axis=1)
    before = jnp.cumsum(present, axis=0) - present
    slot_hit = (
        (present[:, :, None] == 1) & (before[:, :, None] == jnp.arange(cap)[None, None, :])
    ).astype(jnp.int32)
    filled = jnp.sum(slot_hit, axis=0)
    source = jnp.sum(slot_hit * jnp.arange(tok, dtype=jnp.int32)[:, None, None], axis=0)
    picked = jnp.sum(slot_hit.astype(jnp.float32) * table[:, :, None], axis=0)
    source_rep = jnp.repeat(source, SLICES, axis=0).reshape(-1)
    mask = jnp.repeat(filled, SLICES, axis=0).reshape(-1).astype(jnp.float32)[:, None]
    send_rows = (normed[source_rep] * mask.astype(jnp.bfloat16)).reshape(owners, cap, width)
    send_weights = jnp.repeat(picked, SLICES, axis=0).astype(jnp.bfloat16)
    arrived = side_by_side((send_rows, send_weights), "expert", 0, 0, 2)
    result = expert_work(arrived, w_in, w_out)
    returned = lax.all_to_all(result, "expert", split_axis=0, concat_axis=0, tiled=True)
    delta = (
        jnp.zeros((tok, width), jnp.float32)
        .at[source_rep]
        .add(returned.reshape(owners * cap, width).astype(jnp.float32) * mask)
    )
    layer_out = (xf + delta).astype(jnp.bfloat16)
    return from_behind(layer_out[None], "section", 1)


def solution(mesh):
    placed = (
        P("section", "expert", None),
        P("section", "expert", None),
        P("section", "expert", None),
        P("section", None),
        P("section", "expert", None, None),
        P("section", "expert", None),
    )
    return jax.shard_map(
        local, mesh=mesh, in_specs=placed, out_specs=P("section", "expert", None), check_vma=False
    )
```

profile of v0, /device:TPU:24, one launch (start us, length us, event | category | flops | bytes accessed | tf_op | source)
XLA Modules:
  0.0 354.8 jit_solution(8376341761822141627)
XLA Ops:
  0.0 0.8 fusion.12
  0.9 0.1 copy.25
  1.0 0.2 reduce_window_sum.11
  1.1 0.1 copy.26
  1.2 0.2 convert_reduce_fusion.1
  1.5 0.1 reshape_reshape.2
  1.6 1.4 multiply_reduce_fusion
  3.1 0.7 bitcast_convert_fusion.1
  3.8 0.7 select_reduce_fusion.1
  4.5 0.1 fusion.10
  4.6 0.3 copy.27
  4.9 0.8 reduce.1
  5.6 1.5 multiply_convert_fusion
  7.1 5.4 %gather_fusion = bf16[768,3584]{1,0:T(8,128)(2,1)} fusion(bf16[128,3584]{1,0:T(8,128)(2,1)S(1)} %multiply_convert_fusion, s32[1024]{0:T(1024)S(1)} %pad_clamp_fusion), kind=kCustom, calls=%fused_computation | custom fusion | bytes 11013120 | tf_op jit(solution)/shard_map/gather | solution.py:71
  12.5 3.0 broadcast_multiply_fusion
  15.5 0.4 pad_maximum_fusion
  15.9 135.0 %all_to_all.10 = bf16[32,24,3585]{2,1,0:T(8,128)(2,1)S(1)} all-to-all(bf16[32,24,3585]{2,1,0:T(8,128)(2,1)S(1)} %pad_maximum_fusion), channel_id=1, replica_groups=mesh['section'=16,'expert'=32] {'expert'}, dimensions={0} | all-to-all | bytes 11013120 | tf_op jit(solution)/shard_map/all_to_all | solution.py:16
  150.9 2.5 copy-done.1
  153.4 0.2 convert_reduce_fusion
  153.6 0.1 reshape.128
  153.7 2.5 slice-done
  156.2 1.6 fusion.2
  157.8 4.1 %convolution_convert_fusion = bf16[768,3584]{1,0:T(8,128)(2,1)} fusion(bf16[1,128,3584]{2,1,0:T(8,128)(2,1)S(1)} %copy-done.3, f32[768,128,2]{1,0,2:T(8,128)S(1)} %fusion.2, f32[768]{0:T(1024)S(1)} %reshape.128), kind=kOutput, calls=%fused_computation.4 | convolution fusion | flops 708083712 | bytes 7212032 | tf_op jit(solution)/shard_map/dot_general | solution.py:43
  161.9 7.8 %all-to-all-start.1 = ((bf16[32,24,3584]{2,1,0:T(8,128)(2,1)}), bf16[32,24,3584]{2,1,0:T(8,128)(2,1)}, u32[]{:S(2)}, u32[]{:S(2)}) async-start(bf16[32,24,3584]{2,1,0:T(8,128)(2,1)} %bitcast.31), calls=%async_computation.1 | async-start | bytes 11010048 | tf_op jit(solution)/shard_map/all_to_all | solution.py:75
  169.8 0.1 convert_element_type.130
  169.9 1.4 bitcast_convert_fusion
  171.3 123.1 %all-to-all-done.1 = bf16[32,24,3584]{2,1,0:T(8,128)(2,1)} async-done(((bf16[32,24,3584]{2,1,0:T(8,128)(2,1)}), bf16[32,24,3584]{2,1,0:T(8,128)(2,1)}, u32[]{:S(2)}, u32[]{:S(2)}) %all-to-all-start.1) | async-done | bytes 5505056 | tf_op jit(solution)/shard_map/all_to_all | solution.py:75
  294.4 24.9 %scatter_custom_fusion = f32[128,3584]{1,0:T(8,128)} fusion(f32[128,3584]{1,0:T(8,128)} %bitcast_convert_fusion, s32[768]{0:T(1024)S(1)} %fusion.13, bf16[768,3584]{1,0:T(8,128)(2,1)} %bitcast.17, f32[768]{0:T(1024)S(1)} %convert_element_type.130), kind=kCustom, calls=%fused_computation.3 | custom fusion | flops 8257536 | bytes 7344128 | tf_op jit(solution)/shard_map/scatter-add | solution.py:79
  319.3 1.6 convert_bitcast_fusion
  320.9 4.5 %collective-permute-start = (bf16[1,128,3584]{2,1,0:T(8,128)(2,1)S(1)}, bf16[1,128,3584]{2,1,0:T(8,128)(2,1)S(1)}, u32[]{:S(2)}, u32[]{:S(2)}) collective-permute-start(bf16[1,128,3584]{2,1,0:T(8,128)(2,1)S(1)} %convert_bitcast_fusion), channel_id=1, source_target_pairs={{0,32},{32,64},{64,96},{96,128},{128,160},{160,192},{192,224},{224... | collective-permute-start | bytes 2752520 | tf_op jit(solution)/shard_map/ppermute | solution.py:25
  325.4 28.5 %collective-permute-done = bf16[1,128,3584]{2,1,0:T(8,128)(2,1)S(1)} collective-permute-done((bf16[1,128,3584]{2,1,0:T(8,128)(2,1)S(1)}, bf16[1,128,3584]{2,1,0:T(8,128)(2,1)S(1)}, u32[]{:S(2)}, u32[]{:S(2)}) %collective-permute-start) | collective-permute-done | bytes 917536 | tf_op jit(solution)/shard_map/ppermute | solution.py:25
  353.9 0.9 copy.33
  (18 shorter events, 0.1 us)
Async XLA Ops:
  0.0 153.7 %copy-start = (bf16[1,128,2,3584]{3,2,1,0:T(2,128)(2,1)S(1)}, bf16[1,128,2,3584]{3,2,1,0:T(2,128)(2,1)}, u32[]{:S(2)}) copy-start(bf16[1,128,2,3584]{3,2,1,0:T(2,128)(2,1)} %param.10) | copy-start | bytes 5505028
  150.9 2.5 copy-start.1
  153.6 2.6 slice-start
  156.2 1.6 copy-start.3
  161.9 7.9 %copy-start.2 = (bf16[1,128,3584]{2,1,0:T(8,128)(2,1)S(1)}, bf16[1,128,3584]{2,1,0:T(8,128)(2,1)}, u32[]{:S(2)}) copy-start(bf16[1,128,3584]{2,1,0:T(8,128)(2,1)} %param.6) | copy-start | bytes 2752516
  161.9 132.4 %all-to-all-start.1 = ((bf16[32,24,3584]{2,1,0:T(8,128)(2,1)}), bf16[32,24,3584]{2,1,0:T(8,128)(2,1)}, u32[]{:S(2)}, u32[]{:S(2)}) async-start(bf16[32,24,3584]{2,1,0:T(8,128)(2,1)} %bitcast.31), calls=%async_computation.1 | async-start | bytes 11010048 | tf_op jit(solution)/shard_map/all_to_all | solution.py:75
  320.9 33.0 %collective-permute-start = (bf16[1,128,3584]{2,1,0:T(8,128)(2,1)S(1)}, bf16[1,128,3584]{2,1,0:T(8,128)(2,1)S(1)}, u32[]{:S(2)}, u32[]{:S(2)}) collective-permute-start(bf16[1,128,3584]{2,1,0:T(8,128)(2,1)S(1)} %convert_bitcast_fusion), channel_id=1, source_target_pairs={{0,32},{32,64},{64,96},{96,128},{128,160},{160,192},{192,224},{224... | collective-permute-start | bytes 2752520 | tf_op jit(solution)/shard_map/ppermute | solution.py:25
where the time goes:
time: 355 us
  waiting for transfers between devices  152 us (43%)
  blocking collectives  135 us (38%)
  other arithmetic  38 us (11%)
  starting transfers between devices  12.3 us (3%)
  local copies, waits for them, and re-layouts  12.1 us (3%)
  matrix products  5.71 us (2%)
    all_to_all x1, blocking collectives, side_by_side(): lax.all_to_all(both, axis, split_axis=split_dim, concat_axis=concat_dim,...  135 us
    all_to_all x1, waiting for transfers between devices, local(): lax.all_to_all(result, 'expert', split_axis=0, concat_axis=0, tiled=True)  123 us
    ppermute x1, waiting for transfers between devices, from_behind(): lax.ppermute(x, axis, [(i, (i + by) % length) for i in range(length)])  28.5 us
    scatter-add x1, other arithmetic, local(): delta = jnp.zeros((tok, width), jnp.float32).at[source_rep].add(returned....  24.9 us
    all_to_all x1, starting transfers between devices, local(): lax.all_to_all(result, 'expert', split_axis=0, concat_axis=0, tiled=True)  7.81 us
  transfers between devices with their start and end apart: 2, of which 2 were waited for; matrix products, arithmetic and copies ran while one was open for 0% of the time, Pallas kernels for 0%

commit v1 on v0

v1 whole, which is shorter than its diff:
```python
import jax
import jax.numpy as jnp
from jax import lax
from jax.experimental import pallas as pl
from jax.experimental.pallas import tpu as pltpu
from jax.sharding import PartitionSpec as P

CAP = 24
RING = 8
HALF = 4
WIDE = 512
MESH = pl.DeviceIdType.MESH
BF = jnp.bfloat16
F32 = jnp.float32


def relay(
    acts, ids, gates, gain, w_in, w_out,
    out,
    win, wout, resid, table_out, table_in, normed,
    rows, cross, proj, hid, part, came, result,
    local_sem, w_send, w_recv, acts_send, acts_recv, table_send, table_recv,
    cross_send, cross_recv, out_send, out_recv,
    back_send, back_recv, last_send, last_recv,
):
    tok, width = acts.shape
    chunks = width // WIDE
    sec = lax.axis_index("section")
    me = lax.axis_index("expert")
    n_sec = lax.axis_size("section")
    x, y, core = me // 16, (me // 2) % RING, me % 2
    own = y // HALF
    r = y % HALF
    flip = (r >= 2).astype(jnp.int32)
    edge = jnp.logical_or(r == 0, r == 3)
    inner = jnp.logical_not(edge)
    up = 1 - 2 * flip
    far = 1 - own

    def at(col, row, c):
        return col * 16 + row * 2 + c

    def ring(step):
        return at(x, (y + step + RING) % RING, core)

    up_dev, down_dev = ring(up), ring(-up)
    across = at(1 - x, y, core)
    mate = at(x, y, 1 - core)
    after, before = (sec + 1) % n_sec, (sec + n_sec - 1) % n_sec

    def place(p):
        return (own * HALF + 3 * flip + up * p + 2 * RING) % RING

    barrier = pltpu.get_barrier_semaphore()
    partners = [
        (sec, up_dev), (sec, down_dev), (sec, across), (sec, mate),
        (after, me), (after, across), (before, me), (before, across),
    ]
    for who in partners:
        pl.semaphore_signal(barrier, inc=1, device_id=who, device_id_type=MESH)
    pl.semaphore_wait(barrier, len(partners))

    def remote(src, dst, send, recv, who):
        return pltpu.make_async_remote_copy(
            src_ref=src, dst_ref=dst, send_sem=send, recv_sem=recv,
            device_id=who, device_id_type=MESH,
        )

    own_in = pltpu.make_async_copy(w_in, win.at[core], local_sem.at[0])
    own_out = pltpu.make_async_copy(w_out, wout.at[core], local_sem.at[1])
    mate_in = remote(w_in, win.at[core], w_send.at[0], w_recv.at[0], (sec, mate))
    mate_out = remote(w_out, wout.at[core], w_send.at[1], w_recv.at[1], (sec, mate))
    keep = remote(acts, resid, acts_send, acts_recv, (after, me))

    chosen = ids[...]
    weight = gates[...].astype(F32)
    earlier = (
        lax.broadcasted_iota(jnp.int32, (tok, tok), 0)
        < lax.broadcasted_iota(jnp.int32, (tok, tok), 1)
    ).astype(BF)

    def slots(j):
        hit = chosen == j
        present = jnp.max(hit.astype(F32), axis=0, keepdims=True)
        amount = jnp.sum(jnp.where(hit, weight, 0.0), axis=0, keepdims=True)
        count = jnp.dot(
            jnp.broadcast_to(present, (8, tok)).astype(BF), earlier,
            preferred_element_type=F32,
        )[:1]
        index = lax.broadcasted_iota(jnp.int32, (CAP, tok), 0).astype(F32)
        taken = jnp.logical_and(index == count, present > 0.5)
        return taken.astype(F32), amount

    @pl.loop(0, tok // 16)
    def _(i):
        block = pl.ds(pl.multiple_of(i * 16, 16), 16)
        v = acts[block, :].astype(F32)
        mean = jnp.mean(v * v, axis=-1, keepdims=True)
        normed[block, :] = (v * lax.rsqrt(mean + 1e-06) * gain[...]).astype(BF)

    def gather(j, dst):
        pick = slots(j)[0].astype(BF)

        @pl.loop(0, chunks)
        def _(k):
            cols = pl.ds(pl.multiple_of(k * WIDE, WIDE), WIDE)
            dst[:, cols] = jnp.dot(
                pick, normed[:, cols], preferred_element_type=F32
            ).astype(BF)

    for h in range(2):
        gather(2 * (1 - x) + h, cross.at[h])
        remote(
            cross.at[h], rows.at[h, y, 1], cross_send.at[h], cross_recv.at[h],
            (sec, across),
        ).start()
    gather(2 * x + own, rows.at[own, y, 0])
    gather(2 * x + far, rows.at[far, y, 0])

    def push(h, p, i, upward):
        s = place(p)
        d = flip if upward else 1 - flip
        return remote(
            rows.at[h, s, i], rows.at[h, s, i], out_send.at[d, h, s, i],
            out_recv.at[h, s, i], (sec, up_dev if upward else down_dev),
        )

    def got(h, p, i):
        push(h, p, i, True).wait_recv()

    def first(i):
        @pl.when(edge)
        def _():
            push(own, 0, i, True).start()
            push(far, 0, i, False).start()

        @pl.when(inner)
        def _():
            push(own, 1, i, True).start()
            push(far, 1, i, False).start()
            push(own, 1, i, False).start()

    first(0)
    keep.start()
    own_in.start()
    own_out.start()
    mate_in.start()
    mate_out.start()
    for j in range(4):
        taken, amount = slots(j)
        table_out[j] = (taken * amount).astype(BF)
    table = remote(table_out, table_in, table_send, table_recv, (after, me))
    table.start()
    for h in range(2):
        remote(
            cross.at[h], rows.at[h, y, 1], cross_send.at[h], cross_recv.at[h],
            (sec, across),
        ).wait()
    first(1)

    @pl.when(edge)
    def _():
        for p in (7, 1, 6):
            for i in range(2):
                if p == 1:
                    got(far, 1, i)
                    push(far, 1, i, False).start()
                else:
                    got(own, p, i)
                    push(own, p, i, True).start()
        for p in range(1, 6):
            for i in range(2):
                got(own, p, i)

    @pl.when(inner)
    def _():
        for low, high in ((0, 2), (7, 3), (6, 4), (None, 5)):
            for i in range(2):
                if low is not None:
                    got(own, low, i)
                    push(own, low, i, True).start()
                got(own, high, i)
                push(own, high, i, False).start()

    own_in.wait()
    own_out.wait()
    mate_in.wait()
    mate_out.wait()
    total = RING * 2 * CAP

    proj[...] = jnp.zeros_like(proj)

    @pl.loop(0, chunks)
    def _(k):
        cols = pl.ds(pl.multiple_of(k * WIDE, WIDE), WIDE)
        block = rows[own, :, :, :, cols].reshape(total, WIDE)
        for c in range(2):
            proj[c] += lax.dot_general(
                block, win[c, :, cols], (((1,), (1,)), ((), ())),
                preferred_element_type=F32,
            )

    for c in range(2):
        g = proj[c, :, :128]
        u = proj[c, :, 128:]
        hid[:, :, :, c * 128:(c + 1) * 128] = (
            (jax.nn.silu(g) * u).astype(BF).reshape(RING, 2, CAP, 128)
        )

    def work(s):
        @pl.loop(0, chunks)
        def _(k):
            cols = pl.ds(pl.multiple_of(k * WIDE, WIDE), WIDE)
            both = wout[:, :, cols].reshape(256, WIDE)
            for i in range(2):
                part[s, i, :, cols] = jnp.dot(
                    hid[s, i], both, preferred_element_type=F32
                ).astype(BF)

    def back(src, h, p, i, upward):
        s = place(p)
        d = flip if upward else 1 - flip
        return remote(
            src, came.at[d, h, s, i], back_send.at[h, s, i], back_recv.at[d, h, s, i],
            (sec, up_dev if upward else down_dev),
        )

    def arrived(h, p, i, upward):
        s = place(p)
        d = flip if upward else 1 - flip
        box = came.at[d, h, s, i]
        back(box, h, p, i, upward).wait_recv()
        return box

    def add(p, i, box):
        s = place(p)

        @pl.loop(0, chunks)
        def _(k):
            cols = pl.ds(pl.multiple_of(k * WIDE, WIDE), WIDE)
            part[s, i, :, cols] = (
                part[s, i, :, cols].astype(F32) + box[:, cols].astype(F32)
            ).astype(BF)

    def merge(p, i, upward):
        add(p, i, arrived(own, p, i, upward))
        back(part.at[place(p), i], own, p, i, upward).start()

    def deliver(src, h, i):
        return remote(
            src, result.at[2 * x + h], last_send.at[h, i], last_recv.at[2 * x + h],
            (after, me if i == 0 else across),
        )

    @pl.loop(0, RING)
    def _(q):
        pos = (RING + 5 - q) % RING
        s = place(pos)
        work(s)

        @pl.when(jnp.logical_and(edge, jnp.logical_and(pos >= 1, pos <= 5)))
        def _():
            for i in range(2):
                back(part.at[s, i], own, pos, i, True).start()

    @pl.when(edge)
    def _():
        for i in range(2):
            merge(6, i, False)
        for i in range(2):
            merge(7, i, False)
        for i in range(2):
            box = arrived(far, 1, i, True)
            back(box, far, 1, i, True).start()
        for i in range(2):
            add(0, i, arrived(own, 0, i, False))
            deliver(part.at[place(0), i], own, i).start()
        for i in range(2):
            deliver(arrived(far, 0, i, True), far, i).start()

    @pl.when(inner)
    def _():
        for low, high in ((6, 5), (7, 4), (0, 3), (None, 2)):
            for i in range(2):
                merge(high, i, True)
                if low is not None:
                    merge(low, i, False)
        for i in range(2):
            add(1, i, arrived(own, 1, i, True))
            add(1, i, arrived(own, 1, i, False))
            deliver(part.at[place(1), i], own, i).start()
        for i in range(2):
            deliver(arrived(far, 1, i, True), far, i).start()

    keep.wait()
    table.wait()
    for j in range(4):
        remote(
            result.at[j], result.at[j], last_send.at[0, 0], last_recv.at[j], (after, me)
        ).wait_recv()

    @pl.loop(0, chunks)
    def _(k):
        cols = pl.ds(pl.multiple_of(k * WIDE, WIDE), WIDE)
        total = resid[:, cols].astype(F32)
        for j in range(4):
            total += lax.dot_general(
                table_in[j], result[j, :, cols], (((0,), (0,)), ((), ())),
                preferred_element_type=F32,
            )
        out[:, cols] = total.astype(BF)

    for i in range(2):
        @pl.when(edge)
        def _():
            push(own, 0, i, True).wait_send()
            push(far, 0, i, False).wait_send()
            for p in (7, 6):
                push(own, p, i, True).wait_send()
            push(far, 1, i, False).wait_send()
            for p in (1, 2, 3, 4, 5):
                back(part.at[0, 0], own, p, i, True).wait_send()
            for p in (6, 7):
                back(part.at[0, 0], own, p, i, False).wait_send()
            back(part.at[0, 0], far, 1, i, True).wait_send()

        @pl.when(inner)
        def _():
            push(own, 1, i, True).wait_send()
            push(far, 1, i, False).wait_send()
            push(own, 1, i, False).wait_send()
            for p in (0, 7, 6):
                push(own, p, i, True).wait_send()
                back(part.at[0, 0], own, p, i, False).wait_send()
            for p in (2, 3, 4, 5):
                push(own, p, i, False).wait_send()
                back(part.at[0, 0], own, p, i, True).wait_send()

        for h in range(2):
            deliver(part.at[0, 0], h, i).wait_send()


def local(acts, expert_ids, gate_weights, norm_gain, w_in, w_out):
    tok, width = acts.shape[1:]
    hid = w_out.shape[1]
    vmem = pl.BlockSpec(memory_space=pltpu.VMEM)
    hbm = pl.BlockSpec(memory_space=pl.ANY)
    dma = pltpu.SemaphoreType.DMA
    flat_in = w_in[0].transpose(1, 0, 2).reshape(2 * hid, width)
    moved = pl.pallas_call(
        relay,
        out_shape=jax.ShapeDtypeStruct((tok, width), BF),
        in_specs=[vmem, vmem, vmem, vmem, hbm, hbm],
        out_specs=vmem,
        scratch_shapes=[
            pltpu.VMEM((2, 2 * hid, width), BF),
            pltpu.VMEM((2, hid, width), BF),
            pltpu.VMEM((tok, width), BF),
            pltpu.VMEM((4, CAP, tok), BF),
            pltpu.VMEM((4, CAP, tok), BF),
            pltpu.VMEM((tok, width), BF),
            pltpu.VMEM((2, RING, 2, CAP, width), BF),
            pltpu.VMEM((2, CAP, width), BF),
            pltpu.VMEM((2, RING * 2 * CAP, 2 * hid), F32),
            pltpu.VMEM((RING, 2, CAP, 2 * hid), BF),
            pltpu.VMEM((RING, 2, CAP, width), BF),
            pltpu.VMEM((2, 2, RING, 2, CAP, width), BF),
            pltpu.VMEM((4, CAP, width), BF),
            dma((2,)), dma((2,)), dma((2,)), dma, dma, dma, dma,
            dma((2,)), dma((2,)), dma((2, 2, RING, 2)), dma((2, RING, 2)),
            dma((2, RING, 2)), dma((2, 2, RING, 2)), dma((2, 2)), dma((4,)),
        ],
        compiler_params=pltpu.CompilerParams(
            collective_id=0, has_side_effects=True, vmem_limit_bytes=60 * 2**20
        ),
    )(acts[0], expert_ids[0].T, gate_weights[0].T, norm_gain, flat_in, w_out[0])
    return moved[None]


def solution(mesh):
    placed = (
        P("section", "expert", None),
        P("section", "expert", None),
        P("section", "expert", None),
        P("section", None),
        P("section", "expert", None, None),
        P("section", "expert", None),
    )
    return jax.shard_map(
        local, mesh=mesh, in_specs=placed, out_specs=P("section", "expert", None), check_vma=False
    )
```

time: 355 us -> 153 us (0.43)
  the two profiles are of different devices: /device:TPU:24 before, /device:TPU:8 now
where the time goes in v1:
time: 153 us; the launch traced here: 152 us
  Pallas kernels  147 us (96%)
  local copies, waits for them, and re-layouts  5.09 us (3%)
    pallas_call x1, Pallas kernels, local(): pl.pallas_call(relay, out_shape=jax.ShapeDtypeStruct((tok, width), BF), i...  147 us

profile of v1, /device:TPU:8, one launch (start us, length us, event | category | flops | bytes accessed | tf_op | source)
XLA Modules:
  0.0 152.5 jit_solution(15547593134935776922)
XLA Ops:
  0.0 2.9 %copy.7 = bf16[2,128,3584]{2,1,0:T(8,128)(2,1)} copy(bf16[2,128,3584]{2,0,1:T(2,128)(2,1)} %bitcast.15) | data formatting | bytes 3670016 | tf_op jit(solution)/shard_map/transpose | solution.py:349
  2.9 147.4 %shard_map.64 = bf16[128,3584]{1,0:T(8,128)(2,1)} custom-call(bf16[128,3584]{1,0:T(8,128)(2,1)} %bitcast.16, s32[8,128]{1,0:T(8,128)} %bitcast.18, bf16[8,128]{1,0:T(8,128)(2,1)} %bitcast.19, f32[1,3584]{1,0:T(1,128)} %gain.1, bf16[256,3584]{1,0:T(8,128)(2,1)} %bitcast.13, bf16[128,3584]{1,0:T(8,128)(2,1)} %bitcast.17), custom_call_target="tpu_custom_call" | custom-call | tf_op jit(solution)/shard_map/pallas_call | solution.py:350
  150.3 2.2 %copy.9 = bf16[1,128,3584]{2,1,0:T(8,128)(2,1)} copy(bf16[1,128,3584]{2,1,0:T(8,128)(2,1)} %bitcast.14) | data formatting | bytes 1835008

commit v2 on v1

v2 whole, which is shorter than its diff:
```python
import jax
import jax.numpy as jnp
from jax import lax
from jax.experimental import pallas as pl
from jax.experimental.pallas import tpu as pltpu
from jax.sharding import PartitionSpec as P

CAP = 24
RING = 8
HALF = 4
WIDE = 512
MESH = pl.DeviceIdType.MESH
BF = jnp.bfloat16
F32 = jnp.float32
SEND, WORK, ADD, BACK, LAST = range(5)
EDGE = (
    (0, 0, 0, 0, 1), (0, 1, 0, 0, -1), (1, 0, 0, 0, 0), (1, 0, 1, 0, 0), (0, 0, 7, 0, 1),
    (0, 1, 0, 1, -1), (0, 0, 0, 1, 1), (1, 0, 7, 0, 0), (0, 1, 1, 0, -1), (1, 0, 0, 1, 0),
    (0, 0, 6, 0, 1), (0, 1, 1, 1, -1), (1, 0, 6, 0, 0), (0, 0, 7, 1, 1), (1, 0, 7, 1, 0),
    (0, 0, 6, 1, 1), (1, 0, 3, 0, 0), (1, 0, 6, 1, 0), (3, 0, 3, 0, 1), (1, 0, 2, 0, 0),
    (1, 0, 4, 0, 0), (3, 0, 2, 0, 1), (1, 0, 3, 1, 0), (3, 0, 4, 0, 1), (1, 0, 5, 0, 0),
    (3, 0, 5, 0, 1), (1, 0, 4, 1, 0), (3, 0, 4, 1, 1), (1, 0, 5, 1, 0), (3, 0, 5, 1, 1),
    (1, 0, 2, 1, 0), (3, 0, 3, 1, 1), (1, 0, 1, 1, 0), (3, 0, 2, 1, 1), (2, 0, 0, 0, 1),
    (3, 0, 1, 0, 1), (4, 0, 0, 0, 0), (2, 0, 6, 0, 1), (3, 0, 1, 1, 1), (3, 0, 6, 0, -1),
    (2, 0, 7, 0, 1), (3, 0, 7, 0, -1), (4, 1, 0, 0, 0), (2, 0, 6, 1, 1), (3, 0, 6, 1, -1),
    (3, 1, 1, 0, 1), (2, 0, 7, 1, 1), (3, 0, 7, 1, -1), (3, 1, 1, 1, 1), (2, 0, 0, 1, 1),
    (4, 0, 0, 1, 0), (4, 1, 0, 1, 0),
)
INNER = (
    (0, 0, 1, 0, 1), (0, 0, 1, 0, -1), (0, 1, 1, 0, -1), (1, 0, 1, 0, 0), (0, 0, 0, 0, 1),
    (1, 0, 0, 0, 0), (0, 1, 1, 1, -1), (0, 0, 1, 1, 1), (1, 0, 2, 0, 0), (1, 0, 1, 1, 0),
    (0, 0, 3, 0, -1), (0, 0, 7, 0, 1), (0, 0, 2, 0, -1), (1, 0, 3, 0, 0), (0, 0, 0, 1, 1),
    (1, 0, 7, 0, 0), (0, 0, 4, 0, -1), (0, 0, 6, 0, 1), (1, 0, 4, 0, 0), (1, 0, 6, 0, 0),
    (0, 0, 3, 1, -1), (0, 0, 7, 1, 1), (1, 0, 3, 1, 0), (0, 0, 5, 0, -1), (0, 0, 6, 1, 1),
    (1, 0, 5, 0, 0), (1, 0, 6, 1, 0), (0, 0, 4, 1, -1), (2, 0, 3, 0, 1), (1, 0, 4, 1, 0),
    (3, 0, 3, 0, 1), (0, 0, 5, 1, -1), (2, 0, 2, 0, 1), (1, 0, 5, 1, 0), (3, 0, 2, 0, 1),
    (0, 0, 2, 1, -1), (1, 0, 7, 1, 0), (0, 0, 1, 1, -1), (2, 0, 4, 0, 1), (3, 0, 4, 0, 1),
    (2, 0, 0, 0, 1), (1, 0, 2, 1, 0), (3, 0, 0, 0, -1), (2, 0, 5, 0, 1), (1, 0, 0, 1, 0),
    (3, 0, 5, 0, 1), (2, 0, 4, 1, 1), (2, 0, 7, 0, 1), (3, 0, 4, 1, 1), (2, 0, 5, 1, 1),
    (2, 0, 6, 0, 1), (3, 0, 5, 1, 1), (3, 0, 6, 0, -1), (3, 0, 7, 0, -1), (2, 0, 3, 1, 1),
    (2, 0, 7, 1, 1), (3, 0, 3, 1, 1), (2, 0, 2, 1, 1), (2, 0, 6, 1, 1), (3, 0, 2, 1, 1),
    (3, 0, 6, 1, -1), (3, 0, 7, 1, -1), (2, 0, 1, 0, 2), (4, 0, 1, 0, 0), (2, 0, 0, 1, 1),
    (3, 0, 0, 1, -1), (2, 0, 1, 1, 2), (4, 0, 1, 1, 0), (4, 1, 1, 0, 0), (4, 1, 1, 1, 0),
)


def relay(
    acts, ids, gates, gain, w_in, w_out,
    out,
    win, wout, resid, table_out, table_in, normed,
    rows, cross, part, came, result,
    local_sem, w_send, w_recv, acts_send, acts_recv, table_send, table_recv,
    cross_send, cross_recv, out_send, out_recv,
    back_send, back_recv, last_send, last_recv,
):
    tok, width = acts.shape
    chunks = width // WIDE
    sec = lax.axis_index("section")
    me = lax.axis_index("expert")
    n_sec = lax.axis_size("section")
    x, y, core = me // 16, (me // 2) % RING, me % 2
    own = y // HALF
    r = y % HALF
    flip = (r >= 2).astype(jnp.int32)
    edge = jnp.logical_or(r == 0, r == 3)
    inner = jnp.logical_not(edge)
    up = 1 - 2 * flip
    far = 1 - own

    def at(col, row, c):
        return col * 16 + row * 2 + c

    def ring(step):
        return at(x, (y + step + RING) % RING, core)

    up_dev, down_dev = ring(up), ring(-up)
    across = at(1 - x, y, core)
    mate = at(x, y, 1 - core)
    after, before = (sec + 1) % n_sec, (sec + n_sec - 1) % n_sec

    def place(p):
        return (own * HALF + 3 * flip + up * p + 2 * RING) % RING

    barrier = pltpu.get_barrier_semaphore()
    partners = [
        (sec, up_dev), (sec, down_dev), (sec, across), (sec, mate),
        (after, me), (after, across), (before, me), (before, across),
    ]
    for who in partners:
        pl.semaphore_signal(barrier, inc=1, device_id=who, device_id_type=MESH)
    pl.semaphore_wait(barrier, len(partners))

    def remote(src, dst, send, recv, who):
        return pltpu.make_async_remote_copy(
            src_ref=src, dst_ref=dst, send_sem=send, recv_sem=recv,
            device_id=who, device_id_type=MESH,
        )

    own_in = pltpu.make_async_copy(w_in, win.at[core], local_sem.at[0])
    own_out = pltpu.make_async_copy(w_out, wout.at[core], local_sem.at[1])
    mate_in = remote(w_in, win.at[core], w_send.at[0], w_recv.at[0], (sec, mate))
    mate_out = remote(w_out, wout.at[core], w_send.at[1], w_recv.at[1], (sec, mate))
    keep = remote(acts, resid, acts_send, acts_recv, (after, me))

    chosen = ids[...]
    weight = gates[...].astype(F32)
    earlier = (
        lax.broadcasted_iota(jnp.int32, (tok, tok), 0)
        < lax.broadcasted_iota(jnp.int32, (tok, tok), 1)
    ).astype(BF)

    def slots(j):
        hit = chosen == j
        present = jnp.max(hit.astype(F32), axis=0, keepdims=True)
        amount = jnp.sum(jnp.where(hit, weight, 0.0), axis=0, keepdims=True)
        count = jnp.dot(
            jnp.broadcast_to(present, (8, tok)).astype(BF), earlier,
            preferred_element_type=F32,
        )[:1]
        index = lax.broadcasted_iota(jnp.int32, (CAP, tok), 0).astype(F32)
        taken = jnp.logical_and(index == count, present > 0.5)
        return taken.astype(F32), amount

    @pl.loop(0, tok // 16)
    def _(i):
        block = pl.ds(pl.multiple_of(i * 16, 16), 16)
        v = acts[block, :].astype(F32)
        mean = jnp.mean(v * v, axis=-1, keepdims=True)
        normed[block, :] = (v * lax.rsqrt(mean + 1e-06) * gain[...]).astype(BF)

    def gather(j, dst):
        pick = slots(j)[0].astype(BF)

        @pl.loop(0, chunks)
        def _(k):
            cols = pl.ds(pl.multiple_of(k * WIDE, WIDE), WIDE)
            dst[:, cols] = jnp.dot(
                pick, normed[:, cols], preferred_element_type=F32
            ).astype(BF)

    def push(h, p, i, upward):
        s = place(p)
        d = flip if upward else 1 - flip
        return remote(
            rows.at[h, s, i], rows.at[h, s, i], out_send.at[d, h, s, i],
            out_recv.at[h, s, i], (sec, up_dev if upward else down_dev),
        )

    def back(src, h, p, i, upward):
        s = place(p)
        d = flip if upward else 1 - flip
        return remote(
            src, came.at[d, h, s, i], back_send.at[h, s, i], back_recv.at[d, h, s, i],
            (sec, up_dev if upward else down_dev),
        )

    def crossing(h):
        return remote(
            cross.at[h], rows.at[h, y, 1], cross_send.at[h], cross_recv.at[h], (sec, across)
        )

    def deliver(src, h, i):
        return remote(
            src, result.at[2 * x + h], last_send.at[h, i], last_recv.at[2 * x + h],
            (after, me if i == 0 else across),
        )

    def work(s, i):
        def step(k, acc):
            cols = pl.ds(pl.multiple_of(k * WIDE, WIDE), WIDE)
            block = rows[own, s, i, :, cols]
            return tuple(
                acc[c] + lax.dot_general(
                    block, win[c, :, cols], (((1,), (1,)), ((), ())),
                    preferred_element_type=F32,
                )
                for c in range(2)
            )

        zero = jnp.zeros((CAP, 256), F32)
        both = lax.fori_loop(0, chunks, step, (zero, zero))
        hid = jnp.concatenate(
            [(jax.nn.silu(v[:, :128]) * v[:, 128:]).astype(BF) for v in both], axis=1
        )

        @pl.loop(0, chunks)
        def _(k):
            cols = pl.ds(pl.multiple_of(k * WIDE, WIDE), WIDE)
            part[s, i, :, cols] = jnp.dot(
                hid, wout[:, :, cols].reshape(256, WIDE), preferred_element_type=F32
            ).astype(BF)

    def add(s, i, boxes):
        @pl.loop(0, chunks)
        def _(k):
            cols = pl.ds(pl.multiple_of(k * WIDE, WIDE), WIDE)
            total = part[s, i, :, cols].astype(F32)
            for box in boxes:
                total += box[:, cols].astype(F32)
            part[s, i, :, cols] = total.astype(BF)

    sides = (own, far)

    def run(role, ops):
        seen, weights = {(h, role, 0) for h in range(2)}, []

        def need(h, p, i):
            if (h, p, i) in seen:
                return
            seen.add((h, p, i))
            if p == role:
                crossing(sides[h]).wait_recv()
                if {(0, role, 1), (1, role, 1)} <= seen:
                    keep.start()
            else:
                push(sides[h], p, i, True).wait_recv()

        def box(h, p, i, upward):
            d = flip if upward else 1 - flip
            where = came.at[d, sides[h], place(p), i]
            back(where, sides[h], p, i, upward).wait_recv()
            return where

        for kind, h, p, i, way in ops:
            s = place(p)
            if kind == SEND:
                need(h, p, i)
                push(sides[h], p, i, way > 0).start()
            elif kind == WORK:
                need(h, p, i)
                if not weights:
                    weights.append(1)
                    for copy in (own_in, own_out, mate_in, mate_out):
                        copy.wait()
                work(s, i)
            elif kind == ADD:
                if role == 0:
                    ways = [False]
                elif p == 1:
                    ways = [False, True]
                else:
                    ways = [p in (2, 3, 4, 5)]
                add(s, i, [box(h, p, i, w) for w in ways])
            elif kind == BACK:
                src = box(h, p, i, True) if h == 1 else part.at[s, i]
                back(src, sides[h], p, i, way > 0).start()
            else:
                src = box(h, p, i, True) if h == 1 else part.at[s, i]
                deliver(src, sides[h], i).start()
        for kind, h, p, i, way in ops:
            if kind == SEND:
                push(sides[h], p, i, way > 0).wait_send()
            elif kind == BACK:
                back(part.at[0, 0], sides[h], p, i, way > 0).wait_send()
            elif kind == LAST:
                deliver(part.at[0, 0], sides[h], i).wait_send()

    for h in range(2):
        gather(2 * (1 - x) + h, cross.at[h])
        crossing(h).start()
    gather(2 * x + own, rows.at[own, y, 0])
    gather(2 * x + far, rows.at[far, y, 0])
    for j in range(4):
        taken, amount = slots(j)
        table_out[j] = (taken * amount).astype(BF)
    table = remote(table_out, table_in, table_send, table_recv, (after, me))
    table.start()
    own_in.start()
    own_out.start()
    mate_in.start()
    mate_out.start()

    @pl.when(edge)
    def _():
        run(0, EDGE)

    @pl.when(inner)
    def _():
        run(1, INNER)

    keep.wait()
    table.wait()
    for j in range(4):
        remote(
            result.at[j], result.at[j], last_send.at[0, 0], last_recv.at[j], (after, me)
        ).wait_recv()

    @pl.loop(0, chunks)
    def _(k):
        cols = pl.ds(pl.multiple_of(k * WIDE, WIDE), WIDE)
        total = resid[:, cols].astype(F32)
        for j in range(4):
            total += lax.dot_general(
                table_in[j], result[j, :, cols], (((0,), (0,)), ((), ())),
                preferred_element_type=F32,
            )
        out[:, cols] = total.astype(BF)

    for h in range(2):
        crossing(h).wait_send()


def local(acts, expert_ids, gate_weights, norm_gain, w_in, w_out):
    tok, width = acts.shape[1:]
    hid = w_out.shape[1]
    vmem = pl.BlockSpec(memory_space=pltpu.VMEM)
    hbm = pl.BlockSpec(memory_space=pl.ANY)
    dma = pltpu.SemaphoreType.DMA
    flat_in = w_in[0].transpose(1, 0, 2).reshape(2 * hid, width)
    moved = pl.pallas_call(
        relay,
        out_shape=jax.ShapeDtypeStruct((tok, width), BF),
        in_specs=[vmem, vmem, vmem, vmem, hbm, hbm],
        out_specs=vmem,
        scratch_shapes=[
            pltpu.VMEM((2, 2 * hid, width), BF),
            pltpu.VMEM((2, hid, width), BF),
            pltpu.VMEM((tok, width), BF),
            pltpu.VMEM((4, CAP, tok), BF),
            pltpu.VMEM((4, CAP, tok), BF),
            pltpu.VMEM((tok, width), BF),
            pltpu.VMEM((2, RING, 2, CAP, width), BF),
            pltpu.VMEM((2, CAP, width), BF),
            pltpu.VMEM((RING, 2, CAP, width), BF),
            pltpu.VMEM((2, 2, RING, 2, CAP, width), BF),
            pltpu.VMEM((4, CAP, width), BF),
            dma((2,)), dma((2,)), dma((2,)), dma, dma, dma, dma,
            dma((2,)), dma((2,)), dma((2, 2, RING, 2)), dma((2, RING, 2)),
            dma((2, RING, 2)), dma((2, 2, RING, 2)), dma((2, 2)), dma((4,)),
        ],
        compiler_params=pltpu.CompilerParams(
            collective_id=0, has_side_effects=True, vmem_limit_bytes=60 * 2**20
        ),
    )(acts[0], expert_ids[0].T, gate_weights[0].T, norm_gain, flat_in, w_out[0])
    return moved[None]


def solution(mesh):
    placed = (
        P("section", "expert", None),
        P("section", "expert", None),
        P("section", "expert", None),
        P("section", None),
        P("section", "expert", None, None),
        P("section", "expert", None),
    )
    return jax.shard_map(
        local, mesh=mesh, in_specs=placed, out_specs=P("section", "expert", None), check_vma=False
    )
```

time: 153 us -> 123 us (0.80)
  Pallas kernels: 147 us -> 118 us
    pallas_call x1, Pallas kernels: 147 us -> 118 us  [local(): pl.pallas_call(relay, out_shape=jax.ShapeDtypeStruct((tok, width), BF), i...]
where the time goes in v2:
time: 123 us
  Pallas kernels  118 us (96%)
  local copies, waits for them, and re-layouts  5.09 us (4%)
    pallas_call x1, Pallas kernels, local(): pl.pallas_call(relay, out_shape=jax.ShapeDtypeStruct((tok, width), BF), i...  118 us
    transpose x1, local copies, waits for them, and re-layouts, local(): flat_in = w_in[0].transpose(1, 0, 2).reshape(2 * hid, width)  2.93 us

profile of v2, /device:TPU:8, one launch (start us, length us, event | category | flops | bytes accessed | tf_op | source)
XLA Modules:
  0.0 123.2 jit_solution(7707585100085298066)
XLA Ops:
  0.0 2.9 %copy.7 = bf16[2,128,3584]{2,1,0:T(8,128)(2,1)} copy(bf16[2,128,3584]{2,0,1:T(2,128)(2,1)} %bitcast.15) | data formatting | bytes 3670016 | tf_op jit(solution)/shard_map/transpose | solution.py:309
  2.9 118.1 %shard_map.64 = bf16[128,3584]{1,0:T(8,128)(2,1)} custom-call(bf16[128,3584]{1,0:T(8,128)(2,1)} %bitcast.16, s32[8,128]{1,0:T(8,128)} %bitcast.18, bf16[8,128]{1,0:T(8,128)(2,1)} %bitcast.19, f32[1,3584]{1,0:T(1,128)} %gain.1, bf16[256,3584]{1,0:T(8,128)(2,1)} %bitcast.13, bf16[128,3584]{1,0:T(8,128)(2,1)} %bitcast.17), custom_call_target="tpu_custom_call" | custom-call | tf_op jit(solution)/shard_map/pallas_call | solution.py:310
  121.0 2.2 %copy.9 = bf16[1,128,3584]{2,1,0:T(8,128)(2,1)} copy(bf16[1,128,3584]{2,1,0:T(8,128)(2,1)} %bitcast.14) | data formatting | bytes 1835008

commit v3 on v2

--- a/solution.py
+++ b/solution.py
@@ -9,38 +9,39 @@
 RING = 8
 HALF = 4
 WIDE = 512
+HUGE = 1792
 MESH = pl.DeviceIdType.MESH
 BF = jnp.bfloat16
 F32 = jnp.float32
 SEND, WORK, ADD, BACK, LAST = range(5)
 EDGE = (
-    (0, 0, 0, 0, 1), (0, 1, 0, 0, -1), (1, 0, 0, 0, 0), (1, 0, 1, 0, 0), (0, 0, 7, 0, 1),
-    (0, 1, 0, 1, -1), (0, 0, 0, 1, 1), (1, 0, 7, 0, 0), (0, 1, 1, 0, -1), (1, 0, 0, 1, 0),
-    (0, 0, 6, 0, 1), (0, 1, 1, 1, -1), (1, 0, 6, 0, 0), (0, 0, 7, 1, 1), (1, 0, 7, 1, 0),
-    (0, 0, 6, 1, 1), (1, 0, 3, 0, 0), (1, 0, 6, 1, 0), (3, 0, 3, 0, 1), (1, 0, 2, 0, 0),
-    (1, 0, 4, 0, 0), (3, 0, 2, 0, 1), (1, 0, 3, 1, 0), (3, 0, 4, 0, 1), (1, 0, 5, 0, 0),
-    (3, 0, 5, 0, 1), (1, 0, 4, 1, 0), (3, 0, 4, 1, 1), (1, 0, 5, 1, 0), (3, 0, 5, 1, 1),
-    (1, 0, 2, 1, 0), (3, 0, 3, 1, 1), (1, 0, 1, 1, 0), (3, 0, 2, 1, 1), (2, 0, 0, 0, 1),
-    (3, 0, 1, 0, 1), (4, 0, 0, 0, 0), (2, 0, 6, 0, 1), (3, 0, 1, 1, 1), (3, 0, 6, 0, -1),
-    (2, 0, 7, 0, 1), (3, 0, 7, 0, -1), (4, 1, 0, 0, 0), (2, 0, 6, 1, 1), (3, 0, 6, 1, -1),
-    (3, 1, 1, 0, 1), (2, 0, 7, 1, 1), (3, 0, 7, 1, -1), (3, 1, 1, 1, 1), (2, 0, 0, 1, 1),
-    (4, 0, 0, 1, 0), (4, 1, 0, 1, 0),
+    (0, 0, 0, 0, 1), (0, 1, 0, 0, -1), (0, 1, 1, 0, -1), (0, 0, 7, 0, 1), (1, 0, 0, 0, 0),
+    (0, 0, 0, 1, 1), (1, 0, 7, 0, 0), (1, 0, 1, 0, 0), (0, 1, 0, 1, -1), (0, 0, 6, 0, 1),
+    (1, 0, 6, 0, 0), (1, 0, 2, 0, 0), (0, 0, 7, 1, 1), (1, 0, 7, 1, 0), (0, 1, 1, 1, -1),
+    (3, 0, 1, 0, 1), (1, 0, 0, 1, 0), (1, 0, 2, 1, 0), (0, 0, 6, 1, 1), (1, 0, 6, 1, 0),
+    (3, 0, 2, 1, 1), (1, 0, 3, 0, 0), (1, 0, 4, 0, 0), (3, 0, 4, 0, 1), (1, 0, 5, 0, 0),
+    (3, 0, 5, 0, 1), (1, 0, 1, 1, 0), (3, 0, 1, 1, 1), (1, 0, 3, 1, 0), (3, 0, 3, 1, 1),
+    (1, 0, 5, 1, 0), (3, 0, 5, 1, 1), (1, 0, 4, 1, 0), (3, 0, 4, 1, 1), (3, 0, 3, 0, 1),
+    (2, 0, 7, 0, 1), (3, 0, 7, 0, -1), (3, 0, 2, 0, 1), (2, 0, 6, 0, 1), (3, 0, 6, 0, -1),
+    (4, 1, 0, 0, 0), (2, 0, 0, 1, 1), (4, 0, 0, 1, 0), (3, 1, 1, 0, 1), (2, 0, 6, 1, 1),
+    (3, 0, 6, 1, -1), (2, 0, 7, 1, 1), (3, 0, 7, 1, -1), (3, 1, 1, 1, 1), (2, 0, 0, 0, 1),
+    (4, 0, 0, 0, 0), (4, 1, 0, 1, 0),
 )
 INNER = (
-    (0, 0, 1, 0, 1), (0, 0, 1, 0, -1), (0, 1, 1, 0, -1), (1, 0, 1, 0, 0), (0, 0, 0, 0, 1),
-    (1, 0, 0, 0, 0), (0, 1, 1, 1, -1), (0, 0, 1, 1, 1), (1, 0, 2, 0, 0), (1, 0, 1, 1, 0),
-    (0, 0, 3, 0, -1), (0, 0, 7, 0, 1), (0, 0, 2, 0, -1), (1, 0, 3, 0, 0), (0, 0, 0, 1, 1),
-    (1, 0, 7, 0, 0), (0, 0, 4, 0, -1), (0, 0, 6, 0, 1), (1, 0, 4, 0, 0), (1, 0, 6, 0, 0),
-    (0, 0, 3, 1, -1), (0, 0, 7, 1, 1), (1, 0, 3, 1, 0), (0, 0, 5, 0, -1), (0, 0, 6, 1, 1),
-    (1, 0, 5, 0, 0), (1, 0, 6, 1, 0), (0, 0, 4, 1, -1), (2, 0, 3, 0, 1), (1, 0, 4, 1, 0),
-    (3, 0, 3, 0, 1), (0, 0, 5, 1, -1), (2, 0, 2, 0, 1), (1, 0, 5, 1, 0), (3, 0, 2, 0, 1),
-    (0, 0, 2, 1, -1), (1, 0, 7, 1, 0), (0, 0, 1, 1, -1), (2, 0, 4, 0, 1), (3, 0, 4, 0, 1),
-    (2, 0, 0, 0, 1), (1, 0, 2, 1, 0), (3, 0, 0, 0, -1), (2, 0, 5, 0, 1), (1, 0, 0, 1, 0),
-    (3, 0, 5, 0, 1), (2, 0, 4, 1, 1), (2, 0, 7, 0, 1), (3, 0, 4, 1, 1), (2, 0, 5, 1, 1),
-    (2, 0, 6, 0, 1), (3, 0, 5, 1, 1), (3, 0, 6, 0, -1), (3, 0, 7, 0, -1), (2, 0, 3, 1, 1),
-    (2, 0, 7, 1, 1), (3, 0, 3, 1, 1), (2, 0, 2, 1, 1), (2, 0, 6, 1, 1), (3, 0, 2, 1, 1),
-    (3, 0, 6, 1, -1), (3, 0, 7, 1, -1), (2, 0, 1, 0, 2), (4, 0, 1, 0, 0), (2, 0, 0, 1, 1),
-    (3, 0, 0, 1, -1), (2, 0, 1, 1, 2), (4, 0, 1, 1, 0), (4, 1, 1, 0, 0), (4, 1, 1, 1, 0),
+    (0, 0, 1, 0, 1), (0, 1, 1, 0, -1), (0, 0, 1, 0, -1), (0, 0, 0, 0, 1), (0, 0, 2, 0, -1),
+    (1, 0, 1, 0, 0), (0, 0, 1, 1, 1), (1, 0, 0, 0, 0), (1, 0, 1, 1, 0), (0, 1, 1, 1, -1),
+    (0, 0, 7, 0, 1), (1, 0, 7, 0, 0), (1, 0, 2, 0, 0), (0, 0, 2, 1, -1), (0, 0, 0, 1, 1),
+    (1, 0, 0, 1, 0), (0, 0, 3, 0, -1), (1, 0, 2, 1, 0), (0, 0, 6, 0, 1), (0, 0, 4, 0, -1),
+    (1, 0, 6, 0, 0), (1, 0, 4, 0, 0), (0, 0, 7, 1, 1), (1, 0, 7, 1, 0), (1, 0, 3, 2, 0),
+    (0, 0, 5, 0, -1), (0, 0, 1, 1, -1), (1, 0, 5, 0, 0), (0, 0, 6, 1, 1), (1, 0, 6, 1, 0),
+    (0, 0, 3, 1, -1), (1, 0, 4, 1, 0), (2, 0, 2, 1, 1), (3, 0, 2, 1, 1), (0, 0, 5, 1, -1),
+    (1, 0, 5, 1, 0), (2, 0, 4, 0, 1), (3, 0, 4, 0, 1), (0, 0, 4, 1, -1), (2, 0, 5, 0, 1),
+    (3, 0, 5, 0, 1), (2, 0, 7, 0, 1), (3, 0, 7, 0, -1), (2, 0, 1, 1, 2), (4, 0, 1, 1, 0),
+    (2, 0, 6, 0, 1), (3, 0, 6, 0, -1), (2, 0, 3, 1, 1), (3, 0, 3, 1, 1), (2, 0, 5, 1, 1),
+    (3, 0, 5, 1, 1), (2, 0, 0, 1, 1), (3, 0, 0, 1, -1), (2, 0, 4, 1, 1), (3, 0, 4, 1, 1),
+    (2, 0, 6, 1, 1), (3, 0, 6, 1, -1), (2, 0, 3, 0, 1), (3, 0, 3, 0, 1), (2, 0, 7, 1, 1),
+    (3, 0, 7, 1, -1), (2, 0, 2, 0, 1), (3, 0, 2, 0, 1), (2, 0, 0, 0, 1), (3, 0, 0, 0, -1),
+    (4, 1, 1, 0, 0), (2, 0, 1, 0, 2), (4, 0, 1, 0, 0), (4, 1, 1, 1, 0),
 )
 
 
@@ -88,7 +89,6 @@
     ]
     for who in partners:
         pl.semaphore_signal(barrier, inc=1, device_id=who, device_id_type=MESH)
-    pl.semaphore_wait(barrier, len(partners))
 
     def remote(src, dst, send, recv, who):
         return pltpu.make_async_remote_copy(
@@ -165,10 +165,10 @@
             (after, me if i == 0 else across),
         )
 
-    def work(s, i):
+    def work(s, first, count):
         def step(k, acc):
-            cols = pl.ds(pl.multiple_of(k * WIDE, WIDE), WIDE)
-            block = rows[own, s, i, :, cols]
+            cols = pl.ds(pl.multiple_of(k * HUGE, HUGE), HUGE)
+            block = rows[own, s, first:first + count, :, cols].reshape(count * CAP, HUGE)
             return tuple(
                 acc[c] + lax.dot_general(
                     block, win[c, :, cols], (((1,), (1,)), ((), ())),
@@ -177,18 +177,18 @@
                 for c in range(2)
             )
 
-        zero = jnp.zeros((CAP, 256), F32)
-        both = lax.fori_loop(0, chunks, step, (zero, zero))
+        zero = jnp.zeros((count * CAP, 256), F32)
+        both = lax.fori_loop(0, width // HUGE, step, (zero, zero))
         hid = jnp.concatenate(
             [(jax.nn.silu(v[:, :128]) * v[:, 128:]).astype(BF) for v in both], axis=1
         )
 
-        @pl.loop(0, chunks)
+        @pl.loop(0, width // HUGE)
         def _(k):
-            cols = pl.ds(pl.multiple_of(k * WIDE, WIDE), WIDE)
-            part[s, i, :, cols] = jnp.dot(
-                hid, wout[:, :, cols].reshape(256, WIDE), preferred_element_type=F32
-            ).astype(BF)
+            cols = pl.ds(pl.multiple_of(k * HUGE, HUGE), HUGE)
+            part[s, first:first + count, :, cols] = jnp.dot(
+                hid, wout[:, :, cols].reshape(256, HUGE), preferred_element_type=F32
+            ).astype(BF).reshape(count, CAP, HUGE)
 
     def add(s, i, boxes):
         @pl.loop(0, chunks)
@@ -212,6 +212,7 @@
                 crossing(sides[h]).wait_recv()
                 if {(0, role, 1), (1, role, 1)} <= seen:
                     keep.start()
+                    table.start()
             else:
                 push(sides[h], p, i, True).wait_recv()
 
@@ -227,12 +228,14 @@
                 need(h, p, i)
                 push(sides[h], p, i, way > 0).start()
             elif kind == WORK:
-                need(h, p, i)
+                blocks = (0, 1) if i == 2 else (i,)
+                for block in blocks:
+                    need(h, p, block)
                 if not weights:
                     weights.append(1)
                     for copy in (own_in, own_out, mate_in, mate_out):
                         copy.wait()
-                work(s, i)
+                work(s, blocks[0], len(blocks))
             elif kind == ADD:
                 if role == 0:
                     ways = [False]
@@ -255,20 +258,21 @@
             elif kind == LAST:
                 deliver(part.at[0, 0], sides[h], i).wait_send()
 
-    for h in range(2):
-        gather(2 * (1 - x) + h, cross.at[h])
-        crossing(h).start()
+    own_in.start()
+    own_out.start()
+    gather(2 * (1 - x) + own, cross.at[own])
     gather(2 * x + own, rows.at[own, y, 0])
     gather(2 * x + far, rows.at[far, y, 0])
+    gather(2 * (1 - x) + far, cross.at[far])
+    pl.semaphore_wait(barrier, len(partners))
+    for h in (own, far):
+        crossing(h).start()
+    mate_in.start()
+    mate_out.start()
     for j in range(4):
         taken, amount = slots(j)
         table_out[j] = (taken * amount).astype(BF)
     table = remote(table_out, table_in, table_send, table_recv, (after, me))
-    table.start()
-    own_in.start()
-    own_out.start()
-    mate_in.start()
-    mate_out.start()
 
     @pl.when(edge)
     def _():

time: 123 us -> 109 us (0.89)
  Pallas kernels: 118 us -> 104 us
    pallas_call x1, Pallas kernels: 118 us -> 104 us  [local(): pl.pallas_call(relay, out_shape=jax.ShapeDtypeStruct((tok, width), BF), i...]
where the time goes in v3:
time: 109 us
  Pallas kernels  104 us (95%)
  local copies, waits for them, and re-layouts  5.09 us (5%)
    pallas_call x1, Pallas kernels, local(): pl.pallas_call(relay, out_shape=jax.ShapeDtypeStruct((tok, width), BF), i...  104 us
    transpose x1, local copies, waits for them, and re-layouts, local(): flat_in = w_in[0].transpose(1, 0, 2).reshape(2 * hid, width)  2.93 us

profile of v3, /device:TPU:8, one launch (start us, length us, event | category | flops | bytes accessed | tf_op | source)
XLA Modules:
  0.0 109.1 jit_solution(12856766807606679506)
XLA Ops:
  0.0 2.9 %copy.7 = bf16[2,128,3584]{2,1,0:T(8,128)(2,1)} copy(bf16[2,128,3584]{2,0,1:T(2,128)(2,1)} %bitcast.15) | data formatting | bytes 3670016 | tf_op jit(solution)/shard_map/transpose | solution.py:313
  2.9 104.0 %shard_map.64 = bf16[128,3584]{1,0:T(8,128)(2,1)} custom-call(bf16[128,3584]{1,0:T(8,128)(2,1)} %bitcast.16, s32[8,128]{1,0:T(8,128)} %bitcast.18, bf16[8,128]{1,0:T(8,128)(2,1)} %bitcast.19, f32[1,3584]{1,0:T(1,128)} %gain.1, bf16[256,3584]{1,0:T(8,128)(2,1)} %bitcast.13, bf16[128,3584]{1,0:T(8,128)(2,1)} %bitcast.17), custom_call_target="tpu_custom_call" | custom-call | tf_op jit(solution)/shard_map/pallas_call | solution.py:314
  107.0 2.2 %copy.9 = bf16[1,128,3584]{2,1,0:T(8,128)(2,1)} copy(bf16[1,128,3584]{2,1,0:T(8,128)(2,1)} %bitcast.14) | data formatting | bytes 1835008

commit v4 on v3

--- a/solution.py
+++ b/solution.py
@@ -47,9 +47,9 @@
 
 def relay(
     acts, ids, gates, gain, w_in, w_out,
-    out,
-    win, wout, resid, table_out, table_in, normed,
-    rows, cross, part, came, result,
+    resid, table_in, result,
+    win, wout, table_out, normed,
+    rows, cross, part, came,
     local_sem, w_send, w_recv, acts_send, acts_recv, table_send, table_recv,
     cross_send, cross_recv, out_send, out_recv,
     back_send, back_recv, last_send, last_recv,
@@ -102,24 +102,29 @@
     mate_out = remote(w_out, wout.at[core], w_send.at[1], w_recv.at[1], (sec, mate))
     keep = remote(acts, resid, acts_send, acts_recv, (after, me))
 
+    blocks = (2 * (1 - x) + own, 2 * x + own, 2 * x + far, 2 * (1 - x) + far)
     chosen = ids[...]
     weight = gates[...].astype(F32)
+    line = lax.broadcasted_iota(jnp.int32, (4 * CAP, tok), 0)
+    wanted, index = jnp.zeros_like(line), line
+    for k, j in enumerate(blocks):
+        inside = jnp.logical_and(line >= k * CAP, line < (k + 1) * CAP)
+        wanted = jnp.where(inside, j, wanted)
+        index = jnp.where(inside, line - k * CAP, index)
+    present = jnp.zeros((4 * CAP, tok), F32)
+    amount = jnp.zeros((4 * CAP, tok), F32)
+    for k in range(ids.shape[0]):
+        hit = chosen[k:k + 1] == wanted
+        present = jnp.where(hit, 1.0, present)
+        amount = jnp.where(hit, weight[k:k + 1], amount)
     earlier = (
         lax.broadcasted_iota(jnp.int32, (tok, tok), 0)
         < lax.broadcasted_iota(jnp.int32, (tok, tok), 1)
     ).astype(BF)
-
-    def slots(j):
-        hit = chosen == j
-        present = jnp.max(hit.astype(F32), axis=0, keepdims=True)
-        amount = jnp.sum(jnp.where(hit, weight, 0.0), axis=0, keepdims=True)
-        count = jnp.dot(
-            jnp.broadcast_to(present, (8, tok)).astype(BF), earlier,
-            preferred_element_type=F32,
-        )[:1]
-        index = lax.broadcasted_iota(jnp.int32, (CAP, tok), 0).astype(F32)
-        taken = jnp.logical_and(index == count, present > 0.5)
-        return taken.astype(F32), amount
+    count = jnp.dot(present.astype(BF), earlier, preferred_element_type=F32)
+    taken = jnp.where(index.astype(F32) == count, present, 0.0)
+    pick = taken.astype(BF)
+    table_out[...] = (taken * amount).astype(BF)
 
     @pl.loop(0, tok // 16)
     def _(i):
@@ -128,15 +133,13 @@
         mean = jnp.mean(v * v, axis=-1, keepdims=True)
         normed[block, :] = (v * lax.rsqrt(mean + 1e-06) * gain[...]).astype(BF)
 
-    def gather(j, dst):
-        pick = slots(j)[0].astype(BF)
-
-        @pl.loop(0, chunks)
-        def _(k):
-            cols = pl.ds(pl.multiple_of(k * WIDE, WIDE), WIDE)
-            dst[:, cols] = jnp.dot(
-                pick, normed[:, cols], preferred_element_type=F32
-            ).astype(BF)
+    @pl.loop(0, chunks)
+    def _(k):
+        cols = pl.ds(pl.multiple_of(k * WIDE, WIDE), WIDE)
+        packed = jnp.dot(pick, normed[:, cols], preferred_element_type=F32)
+        places = (cross.at[own], rows.at[own, y, 0], rows.at[far, y, 0], cross.at[far])
+        for b, dst in enumerate(places):
+            dst[:, cols] = packed[b * CAP:(b + 1) * CAP].astype(BF)
 
     def push(h, p, i, upward):
         s = place(p)
@@ -159,9 +162,10 @@
             cross.at[h], rows.at[h, y, 1], cross_send.at[h], cross_recv.at[h], (sec, across)
         )
 
-    def deliver(src, h, i):
+    def deliver(src, side, i):
+        b = ((1, 0), (2, 3))[side][i]
         return remote(
-            src, result.at[2 * x + h], last_send.at[h, i], last_recv.at[2 * x + h],
+            src, result.at[b], last_send.at[b], last_recv.at[b],
             (after, me if i == 0 else across),
         )
 
@@ -249,29 +253,22 @@
                 back(src, sides[h], p, i, way > 0).start()
             else:
                 src = box(h, p, i, True) if h == 1 else part.at[s, i]
-                deliver(src, sides[h], i).start()
+                deliver(src, h, i).start()
         for kind, h, p, i, way in ops:
             if kind == SEND:
                 push(sides[h], p, i, way > 0).wait_send()
             elif kind == BACK:
                 back(part.at[0, 0], sides[h], p, i, way > 0).wait_send()
             elif kind == LAST:
-                deliver(part.at[0, 0], sides[h], i).wait_send()
+                deliver(part.at[0, 0], h, i).wait_send()
 
     own_in.start()
     own_out.start()
-    gather(2 * (1 - x) + own, cross.at[own])
-    gather(2 * x + own, rows.at[own, y, 0])
-    gather(2 * x + far, rows.at[far, y, 0])
-    gather(2 * (1 - x) + far, cross.at[far])
     pl.semaphore_wait(barrier, len(partners))
     for h in (own, far):
         crossing(h).start()
     mate_in.start()
     mate_out.start()
-    for j in range(4):
-        taken, amount = slots(j)
-        table_out[j] = (taken * amount).astype(BF)
     table = remote(table_out, table_in, table_send, table_recv, (after, me))
 
     @pl.when(edge)
@@ -284,22 +281,10 @@
 
     keep.wait()
     table.wait()
-    for j in range(4):
+    for b in range(4):
         remote(
-            result.at[j], result.at[j], last_send.at[0, 0], last_recv.at[j], (after, me)
+            result.at[b], result.at[b], last_send.at[b], last_recv.at[b], (after, me)
         ).wait_recv()
-
-    @pl.loop(0, chunks)
-    def _(k):
-        cols = pl.ds(pl.multiple_of(k * WIDE, WIDE), WIDE)
-        total = resid[:, cols].astype(F32)
-        for j in range(4):
-            total += lax.dot_general(
-                table_in[j], result[j, :, cols], (((0,), (0,)), ((), ())),
-                preferred_element_type=F32,
-            )
-        out[:, cols] = total.astype(BF)
-
     for h in range(2):
         crossing(h).wait_send()
 
@@ -311,32 +296,37 @@
     hbm = pl.BlockSpec(memory_space=pl.ANY)
     dma = pltpu.SemaphoreType.DMA
     flat_in = w_in[0].transpose(1, 0, 2).reshape(2 * hid, width)
-    moved = pl.pallas_call(
+    resid, table, result = pl.pallas_call(
         relay,
-        out_shape=jax.ShapeDtypeStruct((tok, width), BF),
+        out_shape=(
+            jax.ShapeDtypeStruct((tok, width), BF),
+            jax.ShapeDtypeStruct((4 * CAP, tok), BF),
+            jax.ShapeDtypeStruct((4, CAP, width), BF),
+        ),
         in_specs=[vmem, vmem, vmem, vmem, hbm, hbm],
-        out_specs=vmem,
+        out_specs=(hbm, hbm, hbm),
         scratch_shapes=[
             pltpu.VMEM((2, 2 * hid, width), BF),
             pltpu.VMEM((2, hid, width), BF),
-            pltpu.VMEM((tok, width), BF),
-            pltpu.VMEM((4, CAP, tok), BF),
-            pltpu.VMEM((4, CAP, tok), BF),
+            pltpu.VMEM((4 * CAP, tok), BF),
             pltpu.VMEM((tok, width), BF),
             pltpu.VMEM((2, RING, 2, CAP, width), BF),
             pltpu.VMEM((2, CAP, width), BF),
             pltpu.VMEM((RING, 2, CAP, width), BF),
             pltpu.VMEM((2, 2, RING, 2, CAP, width), BF),
-            pltpu.VMEM((4, CAP, width), BF),
             dma((2,)), dma((2,)), dma((2,)), dma, dma, dma, dma,
             dma((2,)), dma((2,)), dma((2, 2, RING, 2)), dma((2, RING, 2)),
-            dma((2, RING, 2)), dma((2, 2, RING, 2)), dma((2, 2)), dma((4,)),
+            dma((2, RING, 2)), dma((2, 2, RING, 2)), dma((4,)), dma((4,)),
         ],
         compiler_params=pltpu.CompilerParams(
             collective_id=0, has_side_effects=True, vmem_limit_bytes=60 * 2**20
         ),
     )(acts[0], expert_ids[0].T, gate_weights[0].T, norm_gain, flat_in, w_out[0])
-    return moved[None]
+    delta = lax.dot_general(
+        table, result.reshape(4 * CAP, width), (((0,), (0,)), ((), ())),
+        preferred_element_type=F32,
+    )
+    return (resid.astype(F32) + delta).astype(BF)[None]
 
 
 def solution(mesh):

time: 109 us -> 104 us (0.954)
  Pallas kernels: 104 us -> 98.3 us
  matrix products: 0 us -> 2.76 us
  local copies, waits for them, and re-layouts: 5.09 us -> 2.94 us
    pallas_call x1, Pallas kernels: 104 us -> 98.3 us  [local(): pl.pallas_call(relay, out_shape=(jax.ShapeDtypeStruct((tok, width), BF),...]
    dot_general x0 -> x1, matrix products: none -> 2.76 us  [local(): lax.dot_general(table, result.reshape(4 * CAP, width), (((0,), (0,)), (()...]
    unnamed x1 -> x0, local copies, waits for them, and re-layouts: 2.16 us -> none
where the time goes in v4:
time: 104 us
  Pallas kernels  98.3 us (95%)
  local copies, waits for them, and re-layouts  2.94 us (3%)
  matrix products  2.76 us (3%)
    pallas_call x1, Pallas kernels, local(): pl.pallas_call(relay, out_shape=(jax.ShapeDtypeStruct((tok, width), BF),...  98.3 us
    transpose x1, local copies, waits for them, and re-layouts, local(): flat_in = w_in[0].transpose(1, 0, 2).reshape(2 * hid, width)  2.94 us
    dot_general x1, matrix products, local(): lax.dot_general(table, result.reshape(4 * CAP, width), (((0,), (0,)), (()...  2.76 us

profile of v4, /device:TPU:8, one launch (start us, length us, event | category | flops | bytes accessed | tf_op | source)
XLA Modules:
  0.0 104.0 jit_solution(2570943332018420198)
XLA Ops:
  0.0 2.9 %copy.7 = bf16[2,128,3584]{2,1,0:T(8,128)(2,1)} copy(bf16[2,128,3584]{2,0,1:T(2,128)(2,1)} %bitcast.18) | data formatting | bytes 3670016 | tf_op jit(solution)/shard_map/transpose | solution.py:298
  2.9 98.3 %shard_map.64 = (bf16[128,3584]{1,0:T(8,128)(2,1)}, bf16[96,128]{1,0:T(8,128)(2,1)}, bf16[4,24,3584]{2,1,0:T(8,128)(2,1)}) custom-call(bf16[128,3584]{1,0:T(8,128)(2,1)} %bitcast.19, s32[8,128]{1,0:T(8,128)} %bitcast.22, bf16[8,128]{1,0:T(8,128)(2,1)} %bitcast.23, f32[1,3584]{1,0:T(1,128)} %gain.1, bf16[256,3584]{1,0:T(8,128)(2,1)} %bitcast.17, ...), custom_call_target="tpu_custom_call" | custom-call | tf_op jit(solution)/shard_map/pallas_call | solution.py:299
  101.3 2.8 %fusion.1 = bf16[1,128,3584]{2,1,0:T(8,128)(2,1)} fusion(bf16[96,128]{1,0:T(8,128)(2,1)} %get-tuple-element.9, bf16[96,3584]{1,0:T(8,128)(2,1)} %bitcast.21, bf16[128,3584]{1,0:T(8,128)(2,1)} %get-tuple-element.8), kind=kOutput, calls=%fused_computation.2 | convolution fusion | flops 89456640 | bytes 2547712 | tf_op jit(solution)/shard_map/dot_general | solution.py:325

commit v5 on v4

--- a/solution.py
+++ b/solution.py
@@ -10,6 +10,8 @@
 HALF = 4
 WIDE = 512
 HUGE = 1792
+THIN = 896
+ENDING = {(0, 0, 1, 1), (0, 0, 7, -1), (0, 1, 1, 1), (1, 0, 0, -1), (1, 0, 2, 1)}
 MESH = pl.DeviceIdType.MESH
 BF = jnp.bfloat16
 F32 = jnp.float32
@@ -149,23 +151,28 @@
             out_recv.at[h, s, i], (sec, up_dev if upward else down_dev),
         )
 
-    def back(src, h, p, i, upward):
+    def back(src, h, p, i, upward, k, cols):
         s = place(p)
         d = flip if upward else 1 - flip
         return remote(
-            src, came.at[d, h, s, i], back_send.at[h, s, i], back_recv.at[d, h, s, i],
+            src.at[:, cols], came.at[d, h, s, i, :, cols],
+            back_send.at[h, s, i, k], back_recv.at[d, h, s, i, k],
             (sec, up_dev if upward else down_dev),
         )
+
+    whole = (pl.ds(0, width),)
+    halves = (pl.ds(0, width // 2), pl.ds(width // 2, width // 2))
 
     def crossing(h):
         return remote(
             cross.at[h], rows.at[h, y, 1], cross_send.at[h], cross_recv.at[h], (sec, across)
         )
 
-    def deliver(src, side, i):
+    def deliver(src, side, i, k):
         b = ((1, 0), (2, 3))[side][i]
         return remote(
-            src, result.at[b], last_send.at[b], last_recv.at[b],
+            src.at[:, halves[k]], result.at[b, :, halves[k]],
+            last_send.at[b, k], last_recv.at[b, k],
             (after, me if i == 0 else across),
         )
 
@@ -194,10 +201,10 @@
                 hid, wout[:, :, cols].reshape(256, HUGE), preferred_element_type=F32
             ).astype(BF).reshape(count, CAP, HUGE)
 
-    def add(s, i, boxes):
-        @pl.loop(0, chunks)
+    def add(s, i, boxes, begin, count):
+        @pl.loop(0, count // THIN)
         def _(k):
-            cols = pl.ds(pl.multiple_of(k * WIDE, WIDE), WIDE)
+            cols = pl.ds(pl.multiple_of(begin + k * THIN, 128), THIN)
             total = part[s, i, :, cols].astype(F32)
             for box in boxes:
                 total += box[:, cols].astype(F32)
@@ -220,11 +227,15 @@
             else:
                 push(sides[h], p, i, True).wait_recv()
 
-        def box(h, p, i, upward):
+        def box(h, p, i, upward, k=None):
             d = flip if upward else 1 - flip
             where = came.at[d, sides[h], place(p), i]
-            back(where, sides[h], p, i, upward).wait_recv()
+            cols = whole[0] if k is None else halves[k]
+            back(where, sides[h], p, i, upward, k or 0, cols).wait_recv()
             return where
+
+        def cuts(h, p, way):
+            return halves if (role, h, p, way) in ENDING else whole
 
         for kind, h, p, i, way in ops:
             s = place(p)
@@ -247,20 +258,29 @@
                     ways = [False, True]
                 else:
                     ways = [p in (2, 3, 4, 5)]
-                add(s, i, [box(h, p, i, w) for w in ways])
+                if p == role:
+                    for k in range(2):
+                        boxes = [box(h, p, i, w, k) for w in ways]
+                        add(s, i, boxes, k * (width // 2), width // 2)
+                        deliver(part.at[s, i], h, i, k).start()
+                else:
+                    add(s, i, [box(h, p, i, w) for w in ways], 0, width)
             elif kind == BACK:
                 src = box(h, p, i, True) if h == 1 else part.at[s, i]
-                back(src, sides[h], p, i, way > 0).start()
-            else:
-                src = box(h, p, i, True) if h == 1 else part.at[s, i]
-                deliver(src, h, i).start()
+                for k, cols in enumerate(cuts(h, p, way)):
+                    back(src, sides[h], p, i, way > 0, k, cols).start()
+            elif h == 1:
+                for k in range(2):
+                    deliver(box(h, p, i, True, k), h, i, k).start()
         for kind, h, p, i, way in ops:
             if kind == SEND:
                 push(sides[h], p, i, way > 0).wait_send()
             elif kind == BACK:
-                back(part.at[0, 0], sides[h], p, i, way > 0).wait_send()
+                for k, cols in enumerate(cuts(h, p, way)):
+                    back(part.at[0, 0], sides[h], p, i, way > 0, k, cols).wait_send()
             elif kind == LAST:
-                deliver(part.at[0, 0], h, i).wait_send()
+                for k in range(2):
+                    deliver(part.at[0, 0], h, i, k).wait_send()
 
     own_in.start()
     own_out.start()
@@ -282,9 +302,11 @@
     keep.wait()
     table.wait()
     for b in range(4):
-        remote(
-            result.at[b], result.at[b], last_send.at[b], last_recv.at[b], (after, me)
-        ).wait_recv()
+        for k, cols in enumerate(halves):
+            remote(
+                result.at[b, :, cols], result.at[b, :, cols],
+                last_send.at[b, k], last_recv.at[b, k], (after, me),
+            ).wait_recv()
     for h in range(2):
         crossing(h).wait_send()
 
@@ -316,7 +338,7 @@
             pltpu.VMEM((2, 2, RING, 2, CAP, width), BF),
             dma((2,)), dma((2,)), dma((2,)), dma, dma, dma, dma,
             dma((2,)), dma((2,)), dma((2, 2, RING, 2)), dma((2, RING, 2)),
-            dma((2, RING, 2)), dma((2, 2, RING, 2)), dma((4,)), dma((4,)),
+            dma((2, RING, 2, 2)), dma((2, 2, RING, 2, 2)), dma((4, 2)), dma((4, 2)),
         ],
         compiler_params=pltpu.CompilerParams(
             collective_id=0, has_side_effects=True, vmem_limit_bytes=60 * 2**20

time: 104 us -> 104 us (level)
  no operation moved by 1% of the time
where the time goes in v5:
time: 104 us
  Pallas kernels  98.3 us (95%)
  local copies, waits for them, and re-layouts  2.94 us (3%)
  matrix products  2.75 us (3%)
    pallas_call x1, Pallas kernels, local(): pl.pallas_call(relay, out_shape=(jax.ShapeDtypeStruct((tok, width), BF),...  98.3 us
    transpose x1, local copies, waits for them, and re-layouts, local(): flat_in = w_in[0].transpose(1, 0, 2).reshape(2 * hid, width)  2.94 us
    dot_general x1, matrix products, local(): lax.dot_general(table, result.reshape(4 * CAP, width), (((0,), (0,)), (()...  2.75 us

profile of v5, /device:TPU:8, one launch (start us, length us, event | category | flops | bytes accessed | tf_op | source)
XLA Modules:
  0.0 104.0 jit_solution(11842121815271466180)
XLA Ops:
  0.0 2.9 %copy.7 = bf16[2,128,3584]{2,1,0:T(8,128)(2,1)} copy(bf16[2,128,3584]{2,0,1:T(2,128)(2,1)} %bitcast.18) | data formatting | bytes 3670016 | tf_op jit(solution)/shard_map/transpose | solution.py:320
  2.9 98.3 %shard_map.64 = (bf16[128,3584]{1,0:T(8,128)(2,1)}, bf16[96,128]{1,0:T(8,128)(2,1)}, bf16[4,24,3584]{2,1,0:T(8,128)(2,1)}) custom-call(bf16[128,3584]{1,0:T(8,128)(2,1)} %bitcast.19, s32[8,128]{1,0:T(8,128)} %bitcast.22, bf16[8,128]{1,0:T(8,128)(2,1)} %bitcast.23, f32[1,3584]{1,0:T(1,128)} %gain.1, bf16[256,3584]{1,0:T(8,128)(2,1)} %bitcast.17, ...), custom_call_target="tpu_custom_call" | custom-call | tf_op jit(solution)/shard_map/pallas_call | solution.py:321
  101.2 2.8 %fusion.1 = bf16[1,128,3584]{2,1,0:T(8,128)(2,1)} fusion(bf16[96,128]{1,0:T(8,128)(2,1)} %get-tuple-element.9, bf16[96,3584]{1,0:T(8,128)(2,1)} %bitcast.21, bf16[128,3584]{1,0:T(8,128)(2,1)} %get-tuple-element.8), kind=kOutput, calls=%fused_computation.2 | convolution fusion | flops 89456640 | bytes 2547712 | tf_op jit(solution)/shard_map/dot_general | solution.py:347
